TPU v7x, 32 devices: a whole 2x2x4 slice. The times are simulated.
32 devices in a mesh: dp: 4 (over y, x), ctx: 8 (over z, core).
Axes of the slice: x: 2, y: 2, z: 4, core: 2. Of those that a mesh axis runs over, the one named last changes fastest.
Arguments:
- tokens: bfloat16 [8, 2048, 1024], P('dp', 'ctx'), may hold values from -6 to 6
- positions: int32 [8, 2048], P('dp'), may hold values from 0 to 2047, as said below
- w_query: bfloat16 [1024, 2048], P(('dp', 'ctx')), may hold values from -0.1875 to 0.1875
- w_key: bfloat16 [1024, 1024], P(('dp', 'ctx')), may hold values from -0.1875 to 0.1875
- w_value: bfloat16 [1024, 1024], P(('dp', 'ctx')), may hold values from -0.1875 to 0.1875
- w_out: bfloat16 [2048, 1024], P(('dp', 'ctx')), may hold values from -1 to 1
- w_gate: bfloat16 [1024, 3072], P(('dp', 'ctx')), may hold values from -0.1875 to 0.1875
- w_up: bfloat16 [1024, 3072], P(('dp', 'ctx')), may hold values from -0.1875 to 0.1875
- w_down: bfloat16 [3072, 1024], P(('dp', 'ctx')), may hold values from -0.109375 to 0.109375
- attn_gain: bfloat16 [1024], P(('dp', 'ctx')), may hold values from 0.5 to 1.5
- mlp_gain: bfloat16 [1024], P(('dp', 'ctx')), may hold values from 0.5 to 1.5
- q_gain: bfloat16 [128], P(('dp', 'ctx')), may hold values from 0.5 to 1.5
- k_gain: bfloat16 [128], P(('dp', 'ctx')), may hold values from 0.5 to 1.5
- grad_out: bfloat16 [8, 2048, 1024], P('dp', 'ctx'), may hold values from -6 to 6
Outputs:
- output: bfloat16 [8, 2048, 1024], P('dp', 'ctx')
- input_grad: bfloat16 [8, 2048, 1024], P('dp', 'ctx')
- grad_w_query: float32 [1024, 2048], P(('dp', 'ctx'))
- grad_w_key: float32 [1024, 1024], P(('dp', 'ctx'))
- grad_w_value: float32 [1024, 1024], P(('dp', 'ctx'))
- grad_w_out: float32 [2048, 1024], P(('dp', 'ctx'))
- grad_w_gate: float32 [1024, 3072], P(('dp', 'ctx'))
- grad_w_up: float32 [1024, 3072], P(('dp', 'ctx'))
- grad_w_down: float32 [3072, 1024], P(('dp', 'ctx'))
- grad_attn_gain: float32 [1024], P(('dp', 'ctx'))
- grad_mlp_gain: float32 [1024], P(('dp', 'ctx'))
- grad_q_gain: float32 [128], P(('dp', 'ctx'))
- grad_k_gain: float32 [128], P(('dp', 'ctx'))
Inputs may be any that keep to these rules, and one draw needn't show every extreme that they name: Each row is a permutation of 0 to 2047 made of 16 blocks of 128 consecutive positions in rising order; slots j * 2 * 128 to (j + 1) * 2 * 128 - 1 hold block c followed by block 15 - c, c drawn per row and per j.
All inputs are finite; a program needn't handle non-finite values.
Results may differ from a plain program's by a relative error of at most 0.023.
Values may be sent and summed in bfloat16 or wider, within the bound.
A program may use at most 384 MiB of HBM per device.

v0:
```python
import jax
import jax.numpy as jnp
from jax import lax
from jax.sharding import PartitionSpec as P

H = 16
KV = 8
HD = 128
SEQ = 2048
MICRO = 2
SEQ_MB = 1
EPSILON = 1e-06
THETA = 1000000.0
NEGATIVE = -1e30


def normed(values, weights):
    return values * lax.rsqrt(jnp.mean(values * values, axis=-1, keepdims=True) + EPSILON) * weights


def angle_tables(position_ids):
    half_width = HD // 2
    inverse = THETA ** (-(jnp.arange(half_width).astype(jnp.float32) * 2.0 / HD))
    angles = position_ids.astype(jnp.float32)[:, None] * inverse[None, :]
    angles = jnp.concatenate([angles, angles], axis=-1)
    return (jnp.cos(angles), jnp.sin(angles))


def rotated(values, cosine, sine_table):
    half_width = values.shape[-1] // 2
    turned = jnp.concatenate([-values[..., half_width:], values[..., :half_width]], axis=-1)
    return values * cosine + turned * sine_table


def prepared(raw_rows, gain_vector, cosine, sine_table):
    row_count = raw_rows.shape[0]
    heads = raw_rows.reshape(row_count, -1, HD)
    return rotated(normed(heads, gain_vector), cosine[:, None], sine_table[:, None]).reshape(
        row_count, -1
    )


def scored(query_heads, keys_all, causal):
    result = jnp.einsum(
        "bqkgd,bskd->bkgqs", query_heads, keys_all, preferred_element_type=jnp.float32
    ) * HD ** (-0.5)
    return jnp.where(causal[:, None, None], result, NEGATIVE)


def accumulate(totals, new_items):
    if totals is None:
        return new_items
    return tuple((total_item + new_item for total_item, new_item in zip(totals, new_items)))


def shards(
    tokens,
    positions,
    w_query,
    w_key,
    w_value,
    w_out,
    w_gate,
    w_up,
    w_down,
    attn_gain,
    mlp_gain,
    q_gain,
    k_gain,
    grad_out,
):
    shard_slots = tokens.shape[1]
    model_width = tokens.shape[2]
    ctx_index = lax.axis_index("ctx")
    groups = H // KV
    row_count = SEQ_MB * shard_slots
    attn_totals = None
    mlp_totals = None
    outputs = []
    input_grads = []
    for micro_step in range(MICRO):
        first_seq = micro_step * SEQ_MB
        block_tokens = tokens[first_seq : first_seq + SEQ_MB]
        block_cotangent = grad_out[first_seq : first_seq + SEQ_MB]
        whole_pos = positions[first_seq : first_seq + SEQ_MB]
        own_pos = lax.dynamic_slice_in_dim(whole_pos, ctx_index * shard_slots, shard_slots, 1)
        causal = whole_pos[:, None, :] <= own_pos[:, :, None]
        cosine, sine_table = angle_tables(own_pos.reshape(row_count))
        residual_in = block_tokens.reshape(row_count, model_width).astype(jnp.float32)
        full_query, full_key, full_value, full_out, full_attn_gain, full_q_gain, full_k_gain = (
            lax.all_gather(w_query, ("dp", "ctx"), axis=0, tiled=True),
            lax.all_gather(w_key, ("dp", "ctx"), axis=0, tiled=True),
            lax.all_gather(w_value, ("dp", "ctx"), axis=0, tiled=True),
            lax.all_gather(w_out, ("dp", "ctx"), axis=0, tiled=True),
            lax.all_gather(attn_gain, ("dp", "ctx"), axis=0, tiled=True),
            lax.all_gather(q_gain, ("dp", "ctx"), axis=0, tiled=True),
            lax.all_gather(k_gain, ("dp", "ctx"), axis=0, tiled=True),
        )
        gain_attn = full_attn_gain.astype(jnp.float32)
        query_gain = full_q_gain.astype(jnp.float32)
        key_gain = full_k_gain.astype(jnp.float32)
        hidden = normed(residual_in, gain_attn).astype(jnp.bfloat16)
        query_raw = jnp.dot(hidden, full_query, preferred_element_type=jnp.float32)
        key_raw = jnp.dot(hidden, full_key, preferred_element_type=jnp.float32)
        value_raw = jnp.dot(hidden, full_value, preferred_element_type=jnp.float32)
        queries = prepared(query_raw, query_gain, cosine, sine_table).astype(jnp.bfloat16)
        keys_own = prepared(key_raw, key_gain, cosine, sine_table).astype(jnp.bfloat16)
        values_own = value_raw.astype(jnp.bfloat16)
        keys_all, values_all = (
            lax.all_gather(
                keys_own.reshape(SEQ_MB, shard_slots, KV * HD), "ctx", axis=1, tiled=True
            ),
            lax.all_gather(
                values_own.reshape(SEQ_MB, shard_slots, KV * HD), "ctx", axis=1, tiled=True
            ),
        )
        keys_all = keys_all.reshape(SEQ_MB, SEQ, KV, HD)
        values_all = values_all.reshape(SEQ_MB, SEQ, KV, HD)
        query_heads = queries.reshape(SEQ_MB, shard_slots, KV, groups, HD)
        scores = scored(query_heads, keys_all, causal)
        top_score = jnp.max(scores, axis=-1, keepdims=True)
        log_total = top_score + jnp.log(
            jnp.sum(jnp.exp(scores - top_score), axis=-1, keepdims=True)
        )
        prob_low = jnp.exp(scores - log_total).astype(jnp.bfloat16)
        mixed_heads = jnp.einsum(
            "bkgqs,bskd->bqkgd", prob_low, values_all, preferred_element_type=jnp.float32
        )
        mixed_rows = mixed_heads.reshape(row_count, H * HD).astype(jnp.bfloat16)
        middle = residual_in + jnp.dot(mixed_rows, full_out, preferred_element_type=jnp.float32)
        full_gate, full_up, full_down, full_mlp_gain = (
            lax.all_gather(w_gate, ("dp", "ctx"), axis=0, tiled=True),
            lax.all_gather(w_up, ("dp", "ctx"), axis=0, tiled=True),
            lax.all_gather(w_down, ("dp", "ctx"), axis=0, tiled=True),
            lax.all_gather(mlp_gain, ("dp", "ctx"), axis=0, tiled=True),
        )
        gain_mlp = full_mlp_gain.astype(jnp.float32)
        second = normed(middle, gain_mlp).astype(jnp.bfloat16)
        gate_proj = jnp.dot(second, full_gate, preferred_element_type=jnp.float32)
        up_proj = jnp.dot(second, full_up, preferred_element_type=jnp.float32)
        sigmoid_gate = jax.nn.sigmoid(gate_proj)
        silu_gate = gate_proj * sigmoid_gate
        activated = (silu_gate * up_proj).astype(jnp.bfloat16)
        result_rows = middle + jnp.dot(activated, full_down, preferred_element_type=jnp.float32)
        outputs.append(result_rows.astype(jnp.bfloat16).reshape(SEQ_MB, shard_slots, model_width))
        cotangent = block_cotangent.reshape(row_count, model_width).astype(jnp.float32)
        full_gate, full_up, full_down = (full_gate, full_up, full_down)
        down_grad_in = block_cotangent.reshape(row_count, model_width)
        grad_down_w = jnp.einsum(
            "rf,rd->fd", activated, down_grad_in, preferred_element_type=jnp.float32
        )
        grad_act = jnp.einsum(
            "rd,fd->rf", down_grad_in, full_down, preferred_element_type=jnp.float32
        )
        grad_gate = (
            grad_act * up_proj * sigmoid_gate * (1.0 + gate_proj * (1.0 - sigmoid_gate))
        ).astype(jnp.bfloat16)
        grad_up_rows = (grad_act * silu_gate).astype(jnp.bfloat16)
        grad_gate_w = jnp.einsum("rd,rf->df", second, grad_gate, preferred_element_type=jnp.float32)
        grad_up_w = jnp.einsum(
            "rd,rf->df", second, grad_up_rows, preferred_element_type=jnp.float32
        )
        grad_second = jnp.einsum(
            "rf,df->rd", grad_gate, full_gate, preferred_element_type=jnp.float32
        ) + jnp.einsum("rf,df->rd", grad_up_rows, full_up, preferred_element_type=jnp.float32)
        _, mlp_pull = jax.vjp(normed, middle, gain_mlp)
        grad_middle_part, grad_mlp_gain = mlp_pull(grad_second)
        grad_middle = cotangent + grad_middle_part
        mlp_totals = accumulate(mlp_totals, (grad_gate_w, grad_up_w, grad_down_w, grad_mlp_gain))
        full_query, full_key, full_value, full_out = (full_query, full_key, full_value, full_out)
        attn_grad_in = grad_middle.astype(jnp.bfloat16)
        grad_out_w = jnp.einsum(
            "rh,rd->hd", mixed_rows, attn_grad_in, preferred_element_type=jnp.float32
        )
        grad_mixed = jnp.einsum(
            "rd,hd->rh", attn_grad_in, full_out, preferred_element_type=jnp.float32
        ).astype(jnp.bfloat16)
        grad_heads = grad_mixed.reshape(SEQ_MB, shard_slots, KV, groups, HD)
        scores = scored(query_heads, keys_all, causal)
        weights_full = jnp.exp(scores - log_total)
        grad_probs = jnp.einsum(
            "bqkgd,bskd->bkgqs", grad_heads, values_all, preferred_element_type=jnp.float32
        )
        row_sum = jnp.sum(weights_full * grad_probs, axis=-1, keepdims=True)
        grad_scores = (weights_full * (grad_probs - row_sum)).astype(jnp.bfloat16)
        grad_query = jnp.einsum(
            "bkgqs,bskd->bqkgd", grad_scores, keys_all, preferred_element_type=jnp.float32
        ) * HD ** (-0.5)
        weights_low = weights_full.astype(jnp.bfloat16)
        key_part = jnp.einsum(
            "bkgqs,bqkgd->bskd", grad_scores, query_heads, preferred_element_type=jnp.float32
        ) * HD ** (-0.5)
        value_part = jnp.einsum(
            "bkgqs,bqkgd->bskd", weights_low, grad_heads, preferred_element_type=jnp.float32
        )
        key_sum, value_sum = (
            lax.psum_scatter(
                key_part.reshape(SEQ_MB, SEQ, KV * HD).astype(jnp.bfloat16),
                "ctx",
                scatter_dimension=1,
                tiled=True,
            ).astype(jnp.float32),
            lax.psum_scatter(
                value_part.reshape(SEQ_MB, SEQ, KV * HD).astype(jnp.bfloat16),
                "ctx",
                scatter_dimension=1,
                tiled=True,
            ).astype(jnp.float32),
        )
        _, key_pull = jax.vjp(
            lambda raw_rows, gain_vector: prepared(raw_rows, gain_vector, cosine, sine_table),
            key_raw,
            key_gain,
        )
        grad_key_raw, grad_key_gain = key_pull(key_sum.reshape(row_count, KV * HD))
        _, query_pull = jax.vjp(
            lambda raw_rows, gain_vector: prepared(raw_rows, gain_vector, cosine, sine_table),
            query_raw,
            query_gain,
        )
        grad_query_raw, grad_query_gain = query_pull(grad_query.reshape(row_count, H * HD))
        grad_query_low = grad_query_raw.astype(jnp.bfloat16)
        grad_key_low = grad_key_raw.astype(jnp.bfloat16)
        grad_value_low = value_sum.reshape(row_count, KV * HD).astype(jnp.bfloat16)
        grad_query_w = jnp.einsum(
            "rd,rh->dh", hidden, grad_query_low, preferred_element_type=jnp.float32
        )
        grad_key_w = jnp.einsum(
            "rd,rh->dh", hidden, grad_key_low, preferred_element_type=jnp.float32
        )
        grad_value_w = jnp.einsum(
            "rd,rh->dh", hidden, grad_value_low, preferred_element_type=jnp.float32
        )
        grad_hidden = jnp.einsum(
            "rh,dh->rd", grad_query_low, full_query, preferred_element_type=jnp.float32
        )
        grad_hidden = grad_hidden + jnp.einsum(
            "rh,dh->rd", grad_key_low, full_key, preferred_element_type=jnp.float32
        )
        grad_hidden = grad_hidden + jnp.einsum(
            "rh,dh->rd", grad_value_low, full_value, preferred_element_type=jnp.float32
        )
        _, attn_pull = jax.vjp(normed, residual_in, gain_attn)
        grad_input_part, grad_attn_gain = attn_pull(grad_hidden)
        input_grads.append(
            (grad_middle + grad_input_part)
            .astype(jnp.bfloat16)
            .reshape(SEQ_MB, shard_slots, model_width)
        )
        attn_totals = accumulate(
            attn_totals,
            (
                grad_query_w,
                grad_key_w,
                grad_value_w,
                grad_out_w,
                grad_attn_gain,
                grad_query_gain,
                grad_key_gain,
            ),
        )
    mlp_sums = lax.psum_scatter(mlp_totals, ("dp", "ctx"), scatter_dimension=0, tiled=True)
    attn_sums = lax.psum_scatter(attn_totals, ("dp", "ctx"), scatter_dimension=0, tiled=True)
    output_all = jnp.concatenate(outputs, axis=0)
    input_all = jnp.concatenate(input_grads, axis=0)
    return (
        output_all,
        input_all,
        attn_sums[0],
        attn_sums[1],
        attn_sums[2],
        attn_sums[3],
        mlp_sums[0],
        mlp_sums[1],
        mlp_sums[2],
        attn_sums[4],
        mlp_sums[3],
        attn_sums[5],
        attn_sums[6],
    )


def solution(mesh):
    in_specs = (
        P("dp", "ctx", None),
        P("dp", None),
        P(("dp", "ctx"), None),
        P(("dp", "ctx"), None),
        P(("dp", "ctx"), None),
        P(("dp", "ctx"), None),
        P(("dp", "ctx"), None),
        P(("dp", "ctx"), None),
        P(("dp", "ctx"), None),
        P(("dp", "ctx")),
        P(("dp", "ctx")),
        P(("dp", "ctx")),
        P(("dp", "ctx")),
        P("dp", "ctx", None),
    )
    out_specs = (
        P("dp", "ctx", None),
        P("dp", "ctx", None),
        P(("dp", "ctx"), None),
        P(("dp", "ctx"), None),
        P(("dp", "ctx"), None),
        P(("dp", "ctx"), None),
        P(("dp", "ctx"), None),
        P(("dp", "ctx"), None),
        P(("dp", "ctx"), None),
        P(("dp", "ctx")),
        P(("dp", "ctx")),
        P(("dp", "ctx")),
        P(("dp", "ctx")),
    )
    return jax.shard_map(shards, mesh=mesh, in_specs=in_specs, out_specs=out_specs, check_vma=False)
```

profile of v0, /device:TPU:0, one launch (start us, length us, event | category | flops | bytes accessed | tf_op | source)
XLA Modules:
  0.0 2012.8 jit_solution(11946247957743827104)
XLA Ops:
  12.8 42.3 %all-reduce.17 = (bf16[1024]{0:T(1024)(128)(2,1)S(1)}, bf16[128]{0:T(256)(128)(2,1)S(1)}, bf16[128]{0:T(256)(128)(2,1)S(1)}, bf16[1024]{0:T(1024)(128)(2,1)S(1)}) all-reduce(bf16[1024]{0:T(1024)(128)(2,1)S(1)} %dynamic-update-slice, bf16[128]{0:T(256)(128)(2,1)S(1)} %dynamic-update-slice.1, ...), channel_id=1, replica_groups=mesh['dp'=4,'ctx'=8] {'dp','ctx'}, use_global_device_ids=true, to_apply=%add.8 | all-reduce | flops 2304 | bytes 9216
  79.3 49.3 %all-gather.14.cloned.1.call-done = bf16[1024,1024]{1,0:T(8,128)(2,1)} async-done(((bf16[32,1024]{1,0:T(8,128)(2,1)}), bf16[1024,1024]{1,0:T(8,128)(2,1)}) %all-gather.14.cloned.1.call-update) | async-done | bytes 2097168 | tf_op jit(solution)/shard_map/all_gather | solution.py:93
  140.6 52.0 %all-gather.20.cloned.1.call-done = bf16[1024,2048]{1,0:T(8,128)(2,1)} async-done(((bf16[32,2048]{1,0:T(8,128)(2,1)}), bf16[1024,2048]{1,0:T(8,128)(2,1)}) %all-gather.20.cloned.1.call-update) | async-done | bytes 4194320 | tf_op jit(solution)/shard_map/all_gather | solution.py:91
  208.7 31.7 %all-gather.30.cloned.1.call-done = bf16[1,2048,1024]{1,2,0:T(8,128)(2,1)} async-done(((bf16[1,256,1024]{1,2,0:T(8,128)(2,1)}), bf16[1,2048,1024]{1,2,0:T(8,128)(2,1)}) %all-gather.30.cloned.1.call-update) | async-done | bytes 4194320 | tf_op jit(solution)/shard_map/all_gather | solution.py:110
  293.1 42.1 %all-gather.32.cloned.1.call-done = bf16[2048,1024]{1,0:T(8,128)(2,1)} async-done(((bf16[256,1024]{1,0:T(8,128)(2,1)}), bf16[2048,1024]{1,0:T(8,128)(2,1)}) %all-gather.32.cloned.1.call-update) | async-done | bytes 4194320 | tf_op jit(solution)/shard_map/all_gather | solution.py:113
  340.5 17.6 fusion.39
  358.1 41.0 %all-gather.22.cloned.1.call-done = bf16[2048,1024]{1,0:T(8,128)(2,1)} async-done(((bf16[64,1024]{1,0:T(8,128)(2,1)}), bf16[2048,1024]{1,0:T(8,128)(2,1)}) %all-gather.22.cloned.1.call-update) | async-done | bytes 4194320 | tf_op jit(solution)/shard_map/all_gather | solution.py:94
  403.9 43.2 %all-gather.18.cloned.1.call-done = bf16[1,2048,1024]{1,2,0:T(8,128)(2,1)} async-done(((bf16[1,256,1024]{1,2,0:T(8,128)(2,1)}), bf16[1,2048,1024]{1,2,0:T(8,128)(2,1)}) %all-gather.18.cloned.1.call-update) | async-done | bytes 4194320 | tf_op jit(solution)/shard_map/all_gather | solution.py:110
  477.9 17.2 fusion.36
  499.2 18.6 all-gather.26.cloned.1.call-done
  524.1 64.5 %all-gather.24.cloned.1.call-done = bf16[1024,3072]{1,0:T(8,128)(2,1)} async-done(((bf16[32,3072]{1,0:T(8,128)(2,1)}), bf16[1024,3072]{1,0:T(8,128)(2,1)}) %all-gather.24.cloned.1.call-update) | async-done | bytes 6291472 | tf_op jit(solution)/shard_map/all_gather | solution.py:132
  594.9 64.7 %all-gather.28.cloned.1.call-done = bf16[3072,1024]{1,0:T(8,128)(2,1)} async-done(((bf16[96,1024]{1,0:T(8,128)(2,1)}), bf16[3072,1024]{1,0:T(8,128)(2,1)}) %all-gather.28.cloned.1.call-update) | async-done | bytes 6291472 | tf_op jit(solution)/shard_map/all_gather | solution.py:134
  748.7 25.8 %fusion = (f32[8,2,256]{2,1,0:T(2,128)S(1)}, f32[8,2048,256,2]{2,1,3,0:T(8,128)}) fusion(f32[8,2048,256,2]{2,1,3,0:T(8,128)} %get-tuple-element.100, f32[8,2,256]{2,1,0:T(2,128)S(1)} %bitcast.472, pred[256,2048]{0,1:T(8,128)(4,1)S(1)} %broadcast_compare_fusion, bf16[256,8,2,128]{0,3,2,1:T(8,128)(2,1)S(1)} %bitcast.444, bf16[2048,8,128,1]{2,1,0,3:T(8,128)(2,1)} %bitcast.418), kind=kOutput, calls=%fused_computation.4 | convolution fusion | flops 2189422592 | bytes 72908800 | tf_op jit(solution)/shard_map/bqkgd,bskd->bkgqs/dot_general | solution.py:181
  774.5 28.9 %fusion.13 = bf16[8,2,256,2048]{2,3,1,0:T(8,128)(2,1)} fusion(f32[8,2048,256,2]{2,1,3,0:T(8,128)} %get-tuple-element.112, f32[8,2048,256,2]{2,1,3,0:T(8,128)} %get-tuple-element.100, f32[8,2,256]{2,1,0:T(2,128)S(1)} %get-tuple-element.111, f32[8,2,256]{2,1,0:T(2,128)S(1)} %bitcast.473, pred[256,2048]{0,1:T(8,128)(4,1)S(1)} %broadcast_compare_fusion), kind=kLoop, calls=%fused_computation.23 | loop fusion | flops 50331648 | bytes 84443136 | tf_op jit(solution)/shard_map/reshape.45
  815.1 25.6 %fusion.3 = (f32[8,2,256]{2,1,0:T(2,128)S(1)}, f32[8,2048,256,2]{2,1,3,0:T(8,128)}) fusion(f32[8,2048,256,2]{2,1,3,0:T(8,128)} %get-tuple-element.102, f32[8,2,256]{2,1,0:T(2,128)S(1)} %bitcast.468, pred[256,2048]{0,1:T(8,128)(4,1)S(1)} %broadcast_compare_fusion.1, bf16[256,8,2,128]{0,3,2,1:T(8,128)(2,1)S(1)} %bitcast.442, ...), kind=kOutput, calls=%fused_computation.9 | convolution fusion | flops 2189422592 | bytes 72908800 | tf_op jit(solution)/shard_map/bqkgd,bskd->bkgqs/dot_general | solution.py:181
  840.7 29.0 %fusion.12 = bf16[8,2,256,2048]{2,3,1,0:T(8,128)(2,1)} fusion(f32[8,2048,256,2]{2,1,3,0:T(8,128)} %get-tuple-element.110, f32[8,2048,256,2]{2,1,3,0:T(8,128)} %get-tuple-element.102, f32[8,2,256]{2,1,0:T(2,128)S(1)} %get-tuple-element.109, f32[8,2,256]{2,1,0:T(2,128)S(1)} %bitcast.469, pred[256,2048]{0,1:T(8,128)(4,1)S(1)} %broadcast_compare_fusion.1), kind=kLoop, calls=%fused_computation.22 | loop fusion | flops 50331648 | bytes 84443136 | tf_op jit(solution)/shard_map/reshape.28
  990.5 40.6 %all-reduce.16 = (f32[1024]{0:T(1024)S(1)}, f32[1024]{0:T(1024)S(1)}, f32[128]{0:T(128)S(1)}, f32[128]{0:T(128)S(1)}) all-reduce(f32[1024]{0:T(1024)S(1)} %add.293, f32[1024]{0:T(1024)S(1)} %add.294, f32[128]{0:T(128)S(1)} %add.295, f32[128]{0:T(128)S(1)} %add.296), channel_id=15, replica_groups=mesh['dp'=4,'ctx'=8] {'dp','ctx'}, use_global_device_ids=true, to_apply=%region_35.36.clone | all-reduce | flops 2304 | bytes 18432
  1036.7 45.9 %reduce-scatter.26.cloned.1.call-done = f32[64,1024]{1,0:T(8,128)} async-done(((f32[2048,1024]{1,0:T(8,128)}), f32[64,1024]{1,0:T(8,128)}) %reduce-scatter.26.cloned.1.call-update) | async-done | bytes 262160 | tf_op jit(solution)/shard_map/reduce_scatter | solution.py:263
  1082.6 159.5 %reduce-scatter.30.cloned.1.call-done = f32[32,3072]{1,0:T(8,128)} async-done(((f32[1024,3072]{1,0:T(8,128)}), f32[32,3072]{1,0:T(8,128)}) %reduce-scatter.30.cloned.1.call-update) | async-done | bytes 393232 | tf_op jit(solution)/shard_map/reduce_scatter | solution.py:262
  1242.2 162.3 %reduce-scatter.28.cloned.1.call-done = f32[32,3072]{1,0:T(8,128)} async-done(((f32[1024,3072]{1,0:T(8,128)}), f32[32,3072]{1,0:T(8,128)}) %reduce-scatter.28.cloned.1.call-update) | async-done | bytes 393232 | tf_op jit(solution)/shard_map/reduce_scatter | solution.py:262
  1404.4 161.4 %reduce-scatter.32.cloned.1.call-done = f32[96,1024]{1,0:T(8,128)} async-done(((f32[3072,1024]{1,0:T(8,128)}), f32[96,1024]{1,0:T(8,128)}) %reduce-scatter.32.cloned.1.call-update) | async-done | bytes 393232 | tf_op jit(solution)/shard_map/reduce_scatter | solution.py:262
  1565.8 153.8 %reduce-scatter.20.cloned.1.call-done = f32[32,2048]{1,0:T(8,128)} async-done(((f32[1024,2048]{1,0:T(8,128)}), f32[32,2048]{1,0:T(8,128)}) %reduce-scatter.20.cloned.1.call-update) | async-done | bytes 262160 | tf_op jit(solution)/shard_map/reduce_scatter | solution.py:263
  1719.6 143.8 %reduce-scatter.24.cloned.1.call-done = f32[32,1024]{1,0:T(8,128)} async-done(((f32[1024,1024]{1,0:T(8,128)}), f32[32,1024]{1,0:T(8,128)}) %reduce-scatter.24.cloned.1.call-update) | async-done | bytes 131088 | tf_op jit(solution)/shard_map/reduce_scatter | solution.py:263
  1863.4 142.3 %reduce-scatter.22.cloned.1.call-done = f32[32,1024]{1,0:T(8,128)} async-done(((f32[1024,1024]{1,0:T(8,128)}), f32[32,1024]{1,0:T(8,128)}) %reduce-scatter.22.cloned.1.call-update) | async-done | bytes 131088 | tf_op jit(solution)/shard_map/reduce_scatter | solution.py:263
  (414 shorter events, 393.3 us)
Async XLA Ops:
  7.2 63.1 %all-gather.16.cloned.1.call-start = ((), (), s32[]{:S(2)}) async-start(), calls=%async_computation.12 | async-start | bytes 2162688 | tf_op jit(solution)/shard_map/all_gather | solution.py:92
  7.9 120.7 %all-gather.14.cloned.1.call-start = ((), (), s32[]{:S(2)}) async-start(), calls=%async_computation.11 | async-start | bytes 2162688 | tf_op jit(solution)/shard_map/all_gather | solution.py:93
  8.7 183.9 %all-gather.20.cloned.1.call-start = ((), (), s32[]{:S(2)}) async-start(), calls=%async_computation.14 | async-start | bytes 4325376 | tf_op jit(solution)/shard_map/all_gather | solution.py:91
  9.4 231.0 %all-gather.30.cloned.1.call-start = ((), (), s32[]{:S(2)}) async-start(), calls=%async_computation.19 | async-start | bytes 4718592 | tf_op jit(solution)/shard_map/all_gather | solution.py:110
  79.2 208.7 %all-gather.34.cloned.1.call-start = ((), (), s32[]{:S(2)}) async-start(), calls=%async_computation.32 | async-start | bytes 4718592 | tf_op jit(solution)/shard_map/all_gather | solution.py:113
  131.7 203.5 %all-gather.32.cloned.1.call-start = ((), (), s32[]{:S(2)}) async-start(), calls=%async_computation.31 | async-start | bytes 4718592 | tf_op jit(solution)/shard_map/all_gather | solution.py:113
  135.0 264.1 %all-gather.22.cloned.1.call-start = ((), (), s32[]{:S(2)}) async-start(), calls=%async_computation.15 | async-start | bytes 4325376 | tf_op jit(solution)/shard_map/all_gather | solution.py:94
  135.7 311.3 %all-gather.18.cloned.1.call-start = ((), (), s32[]{:S(2)}) async-start(), calls=%async_computation.13 | async-start | bytes 4718592 | tf_op jit(solution)/shard_map/all_gather | solution.py:110
  137.4 380.4 %all-gather.26.cloned.1.call-start = ((), (), s32[]{:S(2)}) async-start(), calls=%async_computation.17 | async-start | bytes 6488064 | tf_op jit(solution)/shard_map/all_gather | solution.py:133
  138.1 450.5 %all-gather.24.cloned.1.call-start = ((), (), s32[]{:S(2)}) async-start(), calls=%async_computation.16 | async-start | bytes 6488064 | tf_op jit(solution)/shard_map/all_gather | solution.py:132
  138.7 520.9 %all-gather.28.cloned.1.call-start = ((), (), s32[]{:S(2)}) async-start(), calls=%async_computation.18 | async-start | bytes 6488064 | tf_op jit(solution)/shard_map/all_gather | solution.py:134
  139.4 809.5 %reduce-scatter.14.cloned.1.call-start = ((), (), s32[]{:S(2)}) async-start(), calls=%async_computation.21 | async-start | bytes 4718592 | tf_op jit(solution)/shard_map/reduce_scatter | solution.py:203
  207.3 239.8 %copy-start.18 = (bf16[256,16,128]{0,2,1:T(8,128)(2,1)}, bf16[256,16,128]{0,2,1:T(8,128)(2,1)S(1)}, u32[]{:S(2)}) copy-start(bf16[256,16,128]{0,2,1:T(8,128)(2,1)S(1)} %fusion.29) | copy-start | bytes 3145732
  499.0 203.5 %copy-start.11 = (f32[256,1024]{1,0:T(8,128)}, f32[256,1024]{1,0:T(8,128)S(1)}, u32[]{:S(2)}) copy-start(f32[256,1024]{1,0:T(8,128)S(1)} %get-tuple-element.104) | copy-start | bytes 3145732
  726.0 226.8 %reduce-scatter.18.cloned.1.call-start = ((), (), s32[]{:S(2)}) async-start(), calls=%async_computation.23 | async-start | bytes 4718592 | tf_op jit(solution)/shard_map/reduce_scatter | solution.py:203
  748.6 209.7 %reduce-scatter.16.cloned.1.call-start = ((), (), s32[]{:S(2)}) async-start(), calls=%async_computation.22 | async-start | bytes 4718592 | tf_op jit(solution)/shard_map/reduce_scatter | solution.py:197
  813.9 146.8 %reduce-scatter.12.cloned.1.call-start = ((), (), s32[]{:S(2)}) async-start(), calls=%async_computation.20 | async-start | bytes 4718592 | tf_op jit(solution)/shard_map/reduce_scatter | solution.py:197
  880.2 202.4 %reduce-scatter.26.cloned.1.call-start = ((), (), s32[]{:S(2)}) async-start(), calls=%async_computation.27 | async-start | bytes 8650752 | tf_op jit(solution)/shard_map/reduce_scatter | solution.py:263
  887.6 354.6 %reduce-scatter.30.cloned.1.call-start = ((), (), s32[]{:S(2)}) async-start(), calls=%async_computation.29 | async-start | bytes 12976128 | tf_op jit(solution)/shard_map/reduce_scatter | solution.py:262
  897.5 506.9 %reduce-scatter.28.cloned.1.call-start = ((), (), s32[]{:S(2)}) async-start(), calls=%async_computation.28 | async-start | bytes 12976128 | tf_op jit(solution)/shard_map/reduce_scatter | solution.py:262
  907.5 658.3 %reduce-scatter.32.cloned.1.call-start = ((), (), s32[]{:S(2)}) async-start(), calls=%async_computation.30 | async-start | bytes 12976128 | tf_op jit(solution)/shard_map/reduce_scatter | solution.py:262
  917.6 802.0 %reduce-scatter.20.cloned.1.call-start = ((), (), s32[]{:S(2)}) async-start(), calls=%async_computation.24 | async-start | bytes 8650752 | tf_op jit(solution)/shard_map/reduce_scatter | solution.py:263
  948.9 914.6 %reduce-scatter.24.cloned.1.call-start = ((), (), s32[]{:S(2)}) async-start(), calls=%async_computation.26 | async-start | bytes 4325376 | tf_op jit(solution)/shard_map/reduce_scatter | solution.py:263
  958.0 1047.7 %reduce-scatter.22.cloned.1.call-start = ((), (), s32[]{:S(2)}) async-start(), calls=%async_computation.25 | async-start | bytes 4325376 | tf_op jit(solution)/shard_map/reduce_scatter | solution.py:263
  (112 other events, 1820.5 us)
Sparse Core Ops, SparseCore 0:
  11.0 59.1 all-gather.15
  73.2 55.3 all-gather.13
  131.6 60.9 all-gather.19
  194.0 46.3 all-gather.29
  242.5 45.3 all-gather.33
  289.3 45.8 all-gather.31
  338.2 60.8 all-gather.21
  400.7 46.3 all-gather.17
  450.1 67.6 all-gather.25
  520.6 67.9 all-gather.23
  591.6 67.9 all-gather.27
  726.1 48.4 reduce-scatter.13
  776.9 48.1 reduce-scatter.17
  827.3 48.1 reduce-scatter.15
  880.4 49.2 reduce-scatter.11
  932.4 150.2 reduce-scatter.25
  1089.1 153.0 reduce-scatter.29
  1249.7 154.7 reduce-scatter.27
  1411.0 154.7 reduce-scatter.31
  1568.7 150.9 reduce-scatter.19
  1722.6 140.8 reduce-scatter.23
  1866.4 139.3 reduce-scatter.21
where the time goes:
time: 2020 us; the launch traced here: 2010 us
  waiting for transfers between devices  1410 us (70%)
  matrix products  342 us (17%)
  other arithmetic  114 us (6%)
  blocking collectives  82.9 us (4%)
  local copies, waits for them, and re-layouts  47.1 us (2%)
    reduce_scatter x4, waiting for transfers between devices, shards(): lax.psum_scatter(attn_totals, ('dp', 'ctx'), scatter_dimension=0, tiled=T...  486 us
    reduce_scatter x3, waiting for transfers between devices, shards(): lax.psum_scatter(mlp_totals, ('dp', 'ctx'), scatter_dimension=0, tiled=True)  483 us
    unnamed x2, blocking collectives  82.9 us
    all_gather x2, waiting for transfers between devices, shards(): lax.all_gather(keys_own.reshape(SEQ_MB, shard_slots, KV * HD), 'ctx', axi...  74.9 us
    all_gather x1, waiting for transfers between devices, shards(): lax.all_gather(w_down, ('dp', 'ctx'), axis=0, tiled=True)  64.7 us
    all_gather x1, waiting for transfers between devices, shards(): lax.all_gather(w_gate, ('dp', 'ctx'), axis=0, tiled=True)  64.5 us
    all_gather x2, waiting for transfers between devices, shards(): lax.all_gather(values_own.reshape(SEQ_MB, shard_slots, KV * HD), 'ctx', a...  59 us
    another operation x2, other arithmetic  57.9 us
  transfers between devices with their start and end apart: 22, of which 18 were waited for; matrix products, arithmetic and copies ran while one was open for 21% of the time, Pallas kernels for 0%

commit v1 on v0

--- a/solution.py
+++ b/solution.py
@@ -1,7 +1,9 @@
+import functools
 import jax
 import jax.numpy as jnp
 from jax import lax
 from jax.sharding import PartitionSpec as P
+from jax.lax import axis_index, ppermute, psum
 
 H = 16
 KV = 8
@@ -12,6 +14,32 @@
 EPSILON = 1e-06
 THETA = 1000000.0
 NEGATIVE = -1e30
+
+
+def finish_the_windows(view, net_axis):
+    top = psum(1, net_axis)
+    k_now = axis_index(net_axis)
+    shaped, y2, arr_out = (top, k_now, view.shape[1])
+    pool = list(map(lambda nth: (nth, (nth + 1) % shaped), range(shaped)))
+    heap = list(map(lambda nth: (nth, (nth - 1) % shaped), range(shaped)))
+    value_now = jnp.zeros((*view.shape[:1], shaped * arr_out, *view.shape[2:]), view.dtype)
+    side_arr = near = view
+    placed = shaped // 2
+    value_now = lax.dynamic_update_slice_in_dim(value_now, view, y2 * arr_out, axis=1)
+    for j0 in [*range(1, placed + 1)]:
+        side_arr = ppermute(side_arr, net_axis, pool)
+        value_now = lax.dynamic_update_slice_in_dim(
+            value_now, side_arr, (y2 - j0) % shaped * arr_out, axis=1
+        )
+        if j0 < shaped - placed:
+            near = ppermute(near, net_axis, perm=heap)
+            value_now = lax.dynamic_update_slice_in_dim(
+                value_now, near, (y2 + j0) % shaped * arr_out, axis=1
+            )
+    return value_now
+
+
+_pair_clusters = functools.partial(finish_the_windows, net_axis="ctx")
 
 
 def normed(values, weights):
@@ -110,9 +138,7 @@
             lax.all_gather(
                 keys_own.reshape(SEQ_MB, shard_slots, KV * HD), "ctx", axis=1, tiled=True
             ),
-            lax.all_gather(
-                values_own.reshape(SEQ_MB, shard_slots, KV * HD), "ctx", axis=1, tiled=True
-            ),
+            _pair_clusters(values_own.reshape(SEQ_MB, shard_slots, KV * HD)),
         )
         keys_all = keys_all.reshape(SEQ_MB, SEQ, KV, HD)
         values_all = values_all.reshape(SEQ_MB, SEQ, KV, HD)

time: 2020 us -> 1960 us (0.970)
  waiting for transfers between devices: 1410 us -> 1290 us
  local copies, waits for them, and re-layouts: 47.1 us -> 80.9 us
    ppermute x0 -> x14, waiting for transfers between devices: none -> 63.1 us  [the longest x8 35.6 us: finish_the_windows(): side_arr = ppermute(side_arr, net_axis, pool)]
    all_gather x2 -> x0, waiting for transfers between devices: 59 us -> none  [shards(): lax.all_gather(values_own.reshape(SEQ_MB, shard_slots, KV * HD), 'ctx', a...]
    all_gather x1, waiting for transfers between devices: 52 us -> 0.01 us  [shards(): lax.all_gather(w_query, ('dp', 'ctx'), axis=0, tiled=True)]
    all_gather x1, waiting for transfers between devices: 41 us -> 7.65 us  [shards(): lax.all_gather(w_out, ('dp', 'ctx'), axis=0, tiled=True)]
    all_gather x2, waiting for transfers between devices: 74.9 us -> 42.9 us  [shards(): lax.all_gather(keys_own.reshape(SEQ_MB, shard_slots, KV * HD), 'ctx', axi...]
  transfers between devices with their start and end apart: 22 -> 34, of which waited for: 18 -> 22; matrix products, arithmetic and copies ran while one was open for 21% -> 23% of each run, Pallas kernels for 0% -> 0%
where the time goes in v1:
time: 1960 us; the launch traced here: 1940 us
  waiting for transfers between devices  1290 us (66%)
  matrix products  339 us (17%)
  other arithmetic  114 us (6%)
  blocking collectives  82.5 us (4%)
  local copies, waits for them, and re-layouts  80.9 us (4%)
  starting transfers between devices  20.4 us (1%)
    reduce_scatter x4, waiting for transfers between devices, shards(): lax.psum_scatter(attn_totals, ('dp', 'ctx'), scatter_dimension=0, tiled=T...  486 us
    reduce_scatter x3, waiting for transfers between devices, shards(): lax.psum_scatter(mlp_totals, ('dp', 'ctx'), scatter_dimension=0, tiled=True)  483 us
    unnamed x2, blocking collectives  82.5 us
    all_gather x1, waiting for transfers between devices, shards(): lax.all_gather(w_down, ('dp', 'ctx'), axis=0, tiled=True)  64.7 us
    all_gather x1, waiting for transfers between devices, shards(): lax.all_gather(w_gate, ('dp', 'ctx'), axis=0, tiled=True)  64.7 us
    another operation x2, other arithmetic  58.2 us
    dot_general x2, matrix products, shards(): jnp.einsum('bqkgd,bskd->bkgqs', grad_heads, values_all, preferred_element...  50.3 us
    all_gather x1, waiting for transfers between devices, shards(): lax.all_gather(w_value, ('dp', 'ctx'), axis=0, tiled=True)  44.7 us
  transfers between devices with their start and end apart: 34, of which 22 were waited for; matrix products, arithmetic and copies ran while one was open for 23% of the time, Pallas kernels for 0%

profile of v1, /device:TPU:0, one launch (start us, length us, event | category | flops | bytes accessed | tf_op | source)
XLA Modules:
  0.0 1944.9 jit_solution(1017738728960833070)
XLA Ops:
  12.9 42.3 %all-reduce.17 = (bf16[1024]{0:T(1024)(128)(2,1)S(1)}, bf16[128]{0:T(256)(128)(2,1)S(1)}, bf16[128]{0:T(256)(128)(2,1)}, bf16[1024]{0:T(1024)(128)(2,1)}) all-reduce(bf16[1024]{0:T(1024)(128)(2,1)S(1)} %dynamic-update-slice, bf16[128]{0:T(256)(128)(2,1)S(1)} %dynamic-update-slice.1, ...), channel_id=1, replica_groups=mesh['dp'=4,'ctx'=8] {'dp','ctx'}, use_global_device_ids=true, to_apply=%add.8 | all-reduce | flops 2304 | bytes 9216
  83.9 44.7 %all-gather.10.cloned.1.call-done = bf16[1024,1024]{1,0:T(8,128)(2,1)} async-done(((bf16[32,1024]{1,0:T(8,128)(2,1)}), bf16[1024,1024]{1,0:T(8,128)(2,1)}) %all-gather.10.cloned.1.call-update) | async-done | bytes 2097168 | tf_op jit(solution)/shard_map/all_gather | solution.py:121
  277.1 15.5 fusion.9
  307.1 17.5 convolution_convert_fusion.2
  337.1 42.9 %all-gather.14.cloned.1.call-done = bf16[1,2048,1024]{1,2,0:T(8,128)(2,1)} async-done(((bf16[1,256,1024]{1,2,0:T(8,128)(2,1)}), bf16[1,2048,1024]{1,2,0:T(8,128)(2,1)}) %all-gather.14.cloned.1.call-update) | async-done | bytes 4194320 | tf_op jit(solution)/shard_map/all_gather | solution.py:138
  380.0 16.3 fusion.8
  410.8 16.7 convolution_convert_fusion.3
  431.6 19.1 all-gather.22.cloned.1.call-done
  457.0 64.7 %all-gather.20.cloned.1.call-done = bf16[1024,3072]{1,0:T(8,128)(2,1)} async-done(((bf16[32,3072]{1,0:T(8,128)(2,1)}), bf16[1024,3072]{1,0:T(8,128)(2,1)}) %all-gather.20.cloned.1.call-update) | async-done | bytes 6291472 | tf_op jit(solution)/shard_map/all_gather | solution.py:158
  527.9 64.7 %all-gather.24.cloned.1.call-done = bf16[3072,1024]{1,0:T(8,128)(2,1)} async-done(((bf16[96,1024]{1,0:T(8,128)(2,1)}), bf16[3072,1024]{1,0:T(8,128)(2,1)}) %all-gather.24.cloned.1.call-update) | async-done | bytes 6291472 | tf_op jit(solution)/shard_map/all_gather | solution.py:160
  642.4 16.8 bitcast_convert_fusion.1
  665.2 16.6 bitcast_convert_fusion
  681.9 25.2 %fusion = (f32[8,2,256]{2,1,0:T(2,128)S(1)}, f32[8,2048,256,2]{2,1,3,0:T(8,128)}) fusion(f32[8,2048,256,2]{2,1,3,0:T(8,128)} %get-tuple-element.100, f32[8,2,256]{2,1,0:T(2,128)S(1)} %bitcast.480, pred[256,2048]{0,1:T(8,128)(4,1)S(1)} %broadcast_compare_fusion, bf16[2048,8,128,1]{0,2,3,1:T(8,128)(2,1)} %bitcast.28, bf16[256,8,2,128]{0,3,2,1:T(8,128)(2,1)S(1)} %bitcast.454), kind=kOutput, calls=%fused_computation.4 | convolution fusion | flops 2189422592 | bytes 72908800 | tf_op jit(solution)/shard_map/bqkgd,bskd->bkgqs/dot_general | solution.py:207
  707.1 29.1 %fusion.13 = bf16[8,2,256,2048]{2,3,1,0:T(8,128)(2,1)} fusion(f32[8,2048,256,2]{2,1,3,0:T(8,128)} %get-tuple-element.112, f32[8,2048,256,2]{2,1,3,0:T(8,128)} %get-tuple-element.100, f32[8,2,256]{2,1,0:T(2,128)S(1)} %get-tuple-element.111, f32[8,2,256]{2,1,0:T(2,128)S(1)} %bitcast.481, pred[256,2048]{0,1:T(8,128)(4,1)S(1)} %broadcast_compare_fusion), kind=kLoop, calls=%fused_computation.23 | loop fusion | flops 50331648 | bytes 84443136 | tf_op jit(solution)/shard_map/reshape.45
  748.0 25.1 %fusion.3 = (f32[8,2,256]{2,1,0:T(2,128)S(1)}, f32[8,2048,256,2]{2,1,3,0:T(8,128)}) fusion(f32[8,2048,256,2]{2,1,3,0:T(8,128)} %get-tuple-element.102, f32[8,2,256]{2,1,0:T(2,128)S(1)} %bitcast.476, pred[256,2048]{0,1:T(8,128)(4,1)S(1)} %broadcast_compare_fusion.1, bf16[2048,8,128,1]{0,2,3,1:T(8,128)(2,1)} %bitcast.4, bf16[256,8,2,128]{0,3,2,1:T(8,128)(2,1)S(1)} %bitcast.452), kind=kOutput, calls=%fused_computation.9 | convolution fusion | flops 2189422592 | bytes 72908800 | tf_op jit(solution)/shard_map/bqkgd,bskd->bkgqs/dot_general | solution.py:207
  773.1 29.1 %fusion.12 = bf16[8,2,256,2048]{2,3,1,0:T(8,128)(2,1)} fusion(f32[8,2048,256,2]{2,1,3,0:T(8,128)} %get-tuple-element.110, f32[8,2048,256,2]{2,1,3,0:T(8,128)} %get-tuple-element.102, f32[8,2,256]{2,1,0:T(2,128)S(1)} %get-tuple-element.109, f32[8,2,256]{2,1,0:T(2,128)S(1)} %bitcast.477, pred[256,2048]{0,1:T(8,128)(4,1)S(1)} %broadcast_compare_fusion.1), kind=kLoop, calls=%fused_computation.22 | loop fusion | flops 50331648 | bytes 84443136 | tf_op jit(solution)/shard_map/reshape.28
  923.1 40.2 %all-reduce.16 = (f32[1024]{0:T(1024)S(1)}, f32[1024]{0:T(1024)S(1)}, f32[128]{0:T(128)S(1)}, f32[128]{0:T(128)S(1)}) all-reduce(f32[1024]{0:T(1024)S(1)} %add.385, f32[1024]{0:T(1024)S(1)} %add.386, f32[128]{0:T(128)S(1)} %add.387, f32[128]{0:T(128)S(1)} %add.388), channel_id=13, replica_groups=mesh['dp'=4,'ctx'=8] {'dp','ctx'}, use_global_device_ids=true, to_apply=%region_35.36.clone | all-reduce | flops 2304 | bytes 18432
  968.9 46.2 %reduce-scatter.26.cloned.1.call-done = f32[64,1024]{1,0:T(8,128)} async-done(((f32[2048,1024]{1,0:T(8,128)}), f32[64,1024]{1,0:T(8,128)}) %reduce-scatter.26.cloned.1.call-update) | async-done | bytes 262160 | tf_op jit(solution)/shard_map/reduce_scatter | solution.py:289
  1015.1 159.7 %reduce-scatter.30.cloned.1.call-done = f32[32,3072]{1,0:T(8,128)} async-done(((f32[1024,3072]{1,0:T(8,128)}), f32[32,3072]{1,0:T(8,128)}) %reduce-scatter.30.cloned.1.call-update) | async-done | bytes 393232 | tf_op jit(solution)/shard_map/reduce_scatter | solution.py:288
  1174.8 162.0 %reduce-scatter.28.cloned.1.call-done = f32[32,3072]{1,0:T(8,128)} async-done(((f32[1024,3072]{1,0:T(8,128)}), f32[32,3072]{1,0:T(8,128)}) %reduce-scatter.28.cloned.1.call-update) | async-done | bytes 393232 | tf_op jit(solution)/shard_map/reduce_scatter | solution.py:288
  1336.8 161.0 %reduce-scatter.32.cloned.1.call-done = f32[96,1024]{1,0:T(8,128)} async-done(((f32[3072,1024]{1,0:T(8,128)}), f32[96,1024]{1,0:T(8,128)}) %reduce-scatter.32.cloned.1.call-update) | async-done | bytes 393232 | tf_op jit(solution)/shard_map/reduce_scatter | solution.py:288
  1497.8 154.8 %reduce-scatter.20.cloned.1.call-done = f32[32,2048]{1,0:T(8,128)} async-done(((f32[1024,2048]{1,0:T(8,128)}), f32[32,2048]{1,0:T(8,128)}) %reduce-scatter.20.cloned.1.call-update) | async-done | bytes 262160 | tf_op jit(solution)/shard_map/reduce_scatter | solution.py:289
  1652.6 142.8 %reduce-scatter.24.cloned.1.call-done = f32[32,1024]{1,0:T(8,128)} async-done(((f32[1024,1024]{1,0:T(8,128)}), f32[32,1024]{1,0:T(8,128)}) %reduce-scatter.24.cloned.1.call-update) | async-done | bytes 131088 | tf_op jit(solution)/shard_map/reduce_scatter | solution.py:289
  1795.4 142.3 %reduce-scatter.22.cloned.1.call-done = f32[32,1024]{1,0:T(8,128)} async-done(((f32[1024,1024]{1,0:T(8,128)}), f32[32,1024]{1,0:T(8,128)}) %reduce-scatter.22.cloned.1.call-update) | async-done | bytes 131088 | tf_op jit(solution)/shard_map/reduce_scatter | solution.py:289
  (486 shorter events, 432.7 us)
Async XLA Ops:
  7.2 63.1 %all-gather.12.cloned.1.call-start = ((), (), s32[]{:S(2)}) async-start(), calls=%async_computation.12 | async-start | bytes 2162688 | tf_op jit(solution)/shard_map/all_gather | solution.py:120
  7.9 120.7 %all-gather.10.cloned.1.call-start = ((), (), s32[]{:S(2)}) async-start(), calls=%async_computation.11 | async-start | bytes 2162688 | tf_op jit(solution)/shard_map/all_gather | solution.py:121
  8.7 252.4 %all-gather.16.cloned.1.call-start = ((), (), s32[]{:S(2)}) async-start(), calls=%async_computation.14 | async-start | bytes 4325376 | tf_op jit(solution)/shard_map/all_gather | solution.py:119
  9.4 267.7 %all-gather.26.cloned.1.call-start = ((), (), s32[]{:S(2)}) async-start(), calls=%async_computation.19 | async-start | bytes 4718592 | tf_op jit(solution)/shard_map/all_gather | solution.py:138
  79.3 253.0 %all-gather.18.cloned.1.call-start = ((), (), s32[]{:S(2)}) async-start(), calls=%async_computation.15 | async-start | bytes 4325376 | tf_op jit(solution)/shard_map/all_gather | solution.py:122
  79.9 300.2 %all-gather.14.cloned.1.call-start = ((), (), s32[]{:S(2)}) async-start(), calls=%async_computation.13 | async-start | bytes 4718592 | tf_op jit(solution)/shard_map/all_gather | solution.py:138
  81.5 369.2 %all-gather.22.cloned.1.call-start = ((), (), s32[]{:S(2)}) async-start(), calls=%async_computation.17 | async-start | bytes 6488064 | tf_op jit(solution)/shard_map/all_gather | solution.py:159
  82.3 439.4 %all-gather.20.cloned.1.call-start = ((), (), s32[]{:S(2)}) async-start(), calls=%async_computation.16 | async-start | bytes 6488064 | tf_op jit(solution)/shard_map/all_gather | solution.py:158
  83.0 509.6 %all-gather.24.cloned.1.call-start = ((), (), s32[]{:S(2)}) async-start(), calls=%async_computation.18 | async-start | bytes 6488064 | tf_op jit(solution)/shard_map/all_gather | solution.py:160
  83.8 797.6 %reduce-scatter.14.cloned.1.call-start = ((), (), s32[]{:S(2)}) async-start(), calls=%async_computation.21 | async-start | bytes 4718592 | tf_op jit(solution)/shard_map/reduce_scatter | solution.py:229
  142.3 42.8 %collective-permute-start.9 = (bf16[1,256,1024]{2,1,0:T(8,128)(2,1)}, bf16[1,256,1024]{2,1,0:T(8,128)(2,1)}, u32[]{:S(2)}, u32[]{:S(2)}) collective-permute-start(bf16[1,256,1024]{2,1,0:T(8,128)(2,1)} %collective-permute-done.7), channel_id=1, source_target_pairs={{0,1},{1,2},{2,3},{3,4},{4,5},{5,6},{6,7},{7,0},{8,9},{9,10},{10,1... | collective-permute-start | bytes 1572872 | tf_op jit(solution)/shard_map/ppermute | solution.py:30
  188.2 32.9 %collective-permute-start.4 = (bf16[1,256,1024]{2,1,0:T(8,128)(2,1)}, bf16[1,256,1024]{2,1,0:T(8,128)(2,1)}, u32[]{:S(2)}, u32[]{:S(2)}) collective-permute-start(bf16[1,256,1024]{2,1,0:T(8,128)(2,1)} %collective-permute-done.2), channel_id=1, source_target_pairs={{0,1},{1,2},{2,3},{3,4},{4,5},{5,6},{6,7},{7,0},{8,9},{9,10},{10,1... | collective-permute-start | bytes 1572872 | tf_op jit(solution)/shard_map/ppermute | solution.py:30
  202.6 34.5 %collective-permute-start.12 = (bf16[1,256,1024]{2,1,0:T(8,128)(2,1)}, bf16[1,256,1024]{2,1,0:T(8,128)(2,1)}, u32[]{:S(2)}, u32[]{:S(2)}) collective-permute-start(bf16[1,256,1024]{2,1,0:T(8,128)(2,1)} %collective-permute-done.10), channel_id=1, source_target_pairs={{0,7},{1,0},{2,1},{3,2},{4,3},{5,4},{6,5},{7,6},{8,15},{9,8},{10,9... | collective-permute-start | bytes 1572872 | tf_op jit(solution)/shard_map/ppermute | solution.py:35
  221.0 37.9 %collective-permute-start.6 = (bf16[1,256,1024]{2,1,0:T(8,128)(2,1)}, bf16[1,256,1024]{2,1,0:T(8,128)(2,1)}, u32[]{:S(2)}, u32[]{:S(2)}) collective-permute-start(bf16[1,256,1024]{2,1,0:T(8,128)(2,1)} %collective-permute-done.4), channel_id=1, source_target_pairs={{0,1},{1,2},{2,3},{3,4},{4,5},{5,6},{6,7},{7,0},{8,9},{9,10},{10,1... | collective-permute-start | bytes 1572872 | tf_op jit(solution)/shard_map/ppermute | solution.py:30
  659.2 226.1 %reduce-scatter.18.cloned.1.call-start = ((), (), s32[]{:S(2)}) async-start(), calls=%async_computation.23 | async-start | bytes 4718592 | tf_op jit(solution)/shard_map/reduce_scatter | solution.py:229
  681.9 209.0 %reduce-scatter.16.cloned.1.call-start = ((), (), s32[]{:S(2)}) async-start(), calls=%async_computation.22 | async-start | bytes 4718592 | tf_op jit(solution)/shard_map/reduce_scatter | solution.py:223
  746.8 146.4 %reduce-scatter.12.cloned.1.call-start = ((), (), s32[]{:S(2)}) async-start(), calls=%async_computation.20 | async-start | bytes 4718592 | tf_op jit(solution)/shard_map/reduce_scatter | solution.py:223
  812.8 202.4 %reduce-scatter.26.cloned.1.call-start = ((), (), s32[]{:S(2)}) async-start(), calls=%async_computation.27 | async-start | bytes 8650752 | tf_op jit(solution)/shard_map/reduce_scatter | solution.py:289
  820.1 354.8 %reduce-scatter.30.cloned.1.call-start = ((), (), s32[]{:S(2)}) async-start(), calls=%async_computation.29 | async-start | bytes 12976128 | tf_op jit(solution)/shard_map/reduce_scatter | solution.py:288
  830.0 506.8 %reduce-scatter.28.cloned.1.call-start = ((), (), s32[]{:S(2)}) async-start(), calls=%async_computation.28 | async-start | bytes 12976128 | tf_op jit(solution)/shard_map/reduce_scatter | solution.py:288
  840.0 657.8 %reduce-scatter.32.cloned.1.call-start = ((), (), s32[]{:S(2)}) async-start(), calls=%async_computation.30 | async-start | bytes 12976128 | tf_op jit(solution)/shard_map/reduce_scatter | solution.py:288
  850.1 802.5 %reduce-scatter.20.cloned.1.call-start = ((), (), s32[]{:S(2)}) async-start(), calls=%async_computation.24 | async-start | bytes 8650752 | tf_op jit(solution)/shard_map/reduce_scatter | solution.py:289
  881.4 914.0 %reduce-scatter.24.cloned.1.call-start = ((), (), s32[]{:S(2)}) async-start(), calls=%async_computation.26 | async-start | bytes 4325376 | tf_op jit(solution)/shard_map/reduce_scatter | solution.py:289
  890.6 1047.1 %reduce-scatter.22.cloned.1.call-start = ((), (), s32[]{:S(2)}) async-start(), calls=%async_computation.25 | async-start | bytes 4325376 | tf_op jit(solution)/shard_map/reduce_scatter | solution.py:289
  (133 other events, 2891.6 us)
Sparse Core Ops, SparseCore 0:
  11.0 59.2 all-gather.11
  73.2 55.3 all-gather.9
  131.6 68.6 all-gather.15
  202.4 67.3 all-gather.25
  272.6 59.6 all-gather.17
  333.7 46.2 all-gather.13
  383.0 67.6 all-gather.21
  453.7 67.9 all-gather.19
  524.7 67.9 all-gather.23
  659.3 48.4 reduce-scatter.13
  710.1 48.1 reduce-scatter.17
  760.4 48.1 reduce-scatter.15
  812.9 48.9 reduce-scatter.11
  864.5 150.5 reduce-scatter.25
  1021.6 153.2 reduce-scatter.29
  1182.3 154.4 reduce-scatter.27
  1343.3 154.4 reduce-scatter.31
  1500.6 151.9 reduce-scatter.19
  1655.5 139.8 reduce-scatter.23
  1798.2 139.4 reduce-scatter.21
